TPU v7x, 32 devices: a whole 2x2x4 slice. The times are simulated.
32 devices in a mesh: ex: 16 (over z, x, core), feat: 2 (over y).
Axes of the slice: x: 2, y: 2, z: 4, core: 2. Of those that a mesh axis runs over, the one named last changes fastest.
Arguments:
- lanczos_basis: bfloat16 [131072, 384], P(('ex', 'feat')), may hold values from -0.3125 to 0.3125
- diagonal: float32 [131072], P(('ex', 'feat')), may hold values from 0.3 to 9
- lanczos_scale: float32 [384], replicated, may hold values from 0.3 to 3
- test_tiles: int32 [64, 16], replicated, may hold values from 0 to 1023, as said below
- test_values: bfloat16 [64, 16, 128], replicated, may hold values from -6 to 6
- train_tiles: int32 [256, 16], P('ex', 'feat'), may hold values from 0 to 1023, as said below
- train_count: int32 [256, 2], P('ex', 'feat'), may hold values from 1 to 8, as said below
- train_values: bfloat16 [256, 16, 16, 128], P('ex', 'feat'), may hold values from -6 to 6
- resid_weight: float32 [4096], P('ex'), may hold values from -1 to 1
Outputs:
- influence: float32 [64, 4096], P('feat', 'ex')
Inputs may be any that keep to these rules, and one draw needn't show every extreme that they name: `train_tiles`: tile id j lies in the basis rows of the device whose index along ex+feat (ex slowest) is j // 32; the ids in slots f * 8 to (f + 1) * 8 - 1 of a block lie in rows of devices with feat index f. Among all slots of the blocks of one index of ex on one index of feat, at most 12 ids lie in the rows of any one device. In every draw, for each feat index, some device has 12 live slots naming its rows in the blocks of every index of ex. `train_count`: in every draw some block of every index of ex has all 8 slots live on every index of feat. `test_tiles`: the tile ids of one test example are distinct.
All inputs are finite; a program needn't handle non-finite values.
Results may differ from a plain program's by a relative error of at most 0.0042.
Values may be sent and summed in bfloat16 or wider, within the bound.
No kernel may reach another device: no remote copies, remote signals or barrier semaphores. Data moves between devices by JAX's collectives and lax.ppermute only.
A program may use at most 64 MiB of HBM per device.

v0:
```python
import jax
import jax.numpy as jnp
from jax import lax
from jax.sharding import PartitionSpec as P


def body(
    lanczos_basis,
    diagonal,
    lanczos_scale,
    test_tiles,
    test_values,
    train_tiles,
    train_count,
    train_values,
    resid_weight,
):
    ex_devices = lax.axis_size("ex")
    feat_devices = lax.axis_size("feat")
    feat_rows = lanczos_basis.shape[0]
    tiles_here = feat_rows // 128
    test_count = test_tiles.shape[0]
    ex_index = lax.axis_index("ex")
    feat_index = lax.axis_index("feat")
    first_tile = (ex_index * feat_devices + feat_index) * tiles_here
    offsets = test_tiles - first_tile
    matches = (offsets[None, :, :] == jnp.arange(tiles_here)[:, None, None]).astype(jnp.bfloat16)
    local_test = jnp.einsum(
        "ats,tsf->atf", matches, test_values, preferred_element_type=jnp.float32
    ).astype(jnp.bfloat16)
    basis_tiles = lanczos_basis.reshape(tiles_here, 128, lanczos_basis.shape[1])
    partial_proj = jnp.einsum(
        "afr,atf->tr", basis_tiles, local_test, preferred_element_type=jnp.float32
    )
    diag_tiles = diagonal.reshape(tiles_here, 128)
    test_wide = local_test.astype(jnp.float32)
    projection = lax.psum(partial_proj, ("ex", "feat"))
    scaled_proj = (lanczos_scale[None, :] * projection).astype(jnp.bfloat16)
    exact_dir = diag_tiles[:, None, :] * test_wide + jnp.einsum(
        "afr,tr->atf", basis_tiles, scaled_proj, preferred_element_type=jnp.float32
    )
    self_inf = lax.psum(jnp.sum(test_wide * exact_dir, axis=(0, 2)), ("ex", "feat"))
    direction = exact_dir.astype(jnp.bfloat16)
    blocks_here = train_tiles.shape[0]
    slots_here = train_tiles.shape[1]
    slot_total = blocks_here * slots_here
    capacity = max(2, (3 * slot_total + 2 * ex_devices - 1) // (2 * ex_devices))
    flat_ids = train_tiles.reshape(slot_total)
    owners = flat_ids // tiles_here // feat_devices
    local_tile = flat_ids % tiles_here
    slot_live = (jnp.arange(slots_here)[None, :] < train_count).reshape(slot_total)
    onehot = ((owners[:, None] == jnp.arange(ex_devices)[None, :]) & slot_live[:, None]).astype(
        jnp.int32
    )
    slot_rank = jnp.sum(onehot * (jnp.cumsum(onehot, axis=0) - 1), axis=1)
    targets = jnp.where(slot_live, owners, ex_devices)
    requests = (
        jnp.full((ex_devices, capacity), -1, jnp.int32)
        .at[targets, slot_rank]
        .set(local_tile, mode="drop")
    )
    fetched = direction[
        jnp.maximum(lax.all_to_all(requests, "ex", split_axis=0, concat_axis=0, tiled=True), 0)
    ]
    returned = lax.all_to_all(fetched, "ex", split_axis=0, concat_axis=0, tiled=True)
    gathered = jnp.where(
        slot_live[:, None, None], returned[owners, slot_rank], jnp.zeros((), jnp.bfloat16)
    )
    gathered = gathered.reshape(blocks_here, slots_here, test_count, 128)
    partial_scores = jnp.einsum(
        "bjef,bjtf->tbe", train_values, gathered, preferred_element_type=jnp.float32
    ).reshape(test_count, -1)
    tests_here = test_count // feat_devices
    own_scores = lax.psum_scatter(partial_scores, "feat", scatter_dimension=0, tiled=True)
    self_mine = lax.dynamic_slice_in_dim(self_inf, feat_index * tests_here, tests_here)
    return -resid_weight[None, :] * own_scores / jnp.sqrt(self_mine)[:, None]


def solution(mesh):
    return jax.shard_map(
        body,
        mesh=mesh,
        in_specs=(
            P(("ex", "feat"), None),
            P(("ex", "feat")),
            P(),
            P(),
            P(),
            P("ex", "feat"),
            P("ex", "feat"),
            P("ex", "feat", None, None),
            P("ex"),
        ),
        out_specs=P("feat", "ex"),
        check_vma=False,
    )
```

profile of v0, /device:TPU:0, one launch (start us, length us, event | category | flops | bytes accessed | tf_op | source)
XLA Modules:
  0.0 305.9 jit_solution(2954951502102230224)
XLA Ops:
  6.5 0.9 copy.25
  7.4 0.1 reshape.251
  7.5 0.1 reshape.250
  7.6 0.7 iota_compare_fusion.3
  8.4 0.1 lt.83
  8.5 0.1 lt.81
  8.6 0.1 fusion.11
  8.7 0.2 reduce_window_sum.11
  8.9 0.2 select_reduce_fusion
  9.1 0.6 broadcast_in_dim.15
  9.7 18.5 %scatter_fusion = s32[16,12]{1,0:T(8,128)} fusion(s32[16,12]{1,0:T(8,128)} %broadcast_in_dim.15, s32[128]{0:T(128)S(1)} %fusion.21, s32[128]{0:T(128)S(1)} %get-tuple-element.9), kind=kCustom, calls=%fused_computation.2 | custom fusion | bytes 2560 | tf_op jit(solution)/shard_map/scatter | solution.py:60
  28.2 7.1 %all-to-all-start = ((s32[16,1,12]{2,1,0:T(1,128)}), s32[16,1,12]{2,1,0:T(1,128)S(1)}, u32[]{:S(2)}, u32[]{:S(2)}) async-start(s32[16,1,12]{2,1,0:T(1,128)} %bitcast.10), calls=%async_computation | async-start | bytes 16384 | tf_op jit(solution)/shard_map/all_to_all | solution.py:63
  35.4 0.7 broadcast_subtract_fusion
  36.1 0.1 copy.22
  36.2 1.6 fusion.3
  37.8 0.8 copy-done.1
  38.6 1.3 convolution_bitcast_fusion
  39.9 0.0 reduce-scatter.2.cloned.1.call-start
  39.9 1.8 all-to-all-done
  41.7 0.1 reshape.255
  41.8 124.3 %all-reduce.2.cloned.1.call-done = f32[64,384]{1,0:T(8,128)} async-done(((f32[64,384]{1,0:T(8,128)}), f32[64,384]{1,0:T(8,128)}) %all-reduce.2.cloned.1.call-update) | async-done | bytes 98320 | tf_op jit(solution)/shard_map/psum | solution.py:37
  166.1 2.0 fusion.13
  168.2 0.8 fusion.5
  169.0 1.0 copy.28
  170.0 3.8 %gather_fusion = bf16[192,64,128]{2,1,0:T(8,128)(2,1)} fusion(bf16[32,64,128]{2,1,0:T(8,128)(2,1)} %copy.28, s32[1024]{0:T(1024)S(1)} %pad_clamp_fusion), kind=kCustom, calls=%fused_computation | custom fusion | bytes 6292224 | tf_op jit(solution)/shard_map/gather | solution.py:62
  173.8 76.2 %all_to_all.14 = bf16[16,12,64,128]{3,2,1,0:T(8,128)(2,1)} all-to-all(bf16[16,12,64,128]{3,2,1,0:T(8,128)(2,1)} %bitcast.43), channel_id=1, replica_groups=mesh['ex'=16,'feat'=2] {'ex'}, dimensions={0} | all-to-all | bytes 6291456 | tf_op jit(solution)/shard_map/all_to_all | solution.py:65
  250.0 4.2 %gather_fusion.1 = bf16[128,64,128]{2,1,0:T(8,128)(2,1)} fusion(bf16[16,12,64,128]{3,2,1,0:T(8,128)(2,1)} %all_to_all.14, s32[128]{0:T(128)S(1)} %get-tuple-element.5), kind=kCustom, calls=%fused_computation.1 | custom fusion | bytes 4195328 | tf_op jit(solution)/shard_map/gather | solution.py:67
  254.2 2.4 fusion
  256.6 0.7 copy.29
  257.4 40.1 %psum.15 = f32[64]{0:T(128)S(1)} all-reduce(f32[64]{0:T(128)S(1)} %get-tuple-element.7), channel_id=1, replica_groups=mesh['ex'=16,'feat'=2] {'ex','feat'}, use_global_device_ids=true, to_apply=%region_6.7 | all-reduce | flops 64 | bytes 512 | tf_op jit(solution)/shard_map/psum | solution.py:42
  297.5 0.1 dynamic-slice_sqrt_fusion
  297.6 1.5 multiply_divide_fusion
  (21 shorter events, 0.2 us)
Async XLA Ops:
  6.5 31.2 %copy-start = (bf16[4096,384]{1,0:T(8,128)(2,1)S(1)}, bf16[4096,384]{1,0:T(8,128)(2,1)}, u32[]{:S(2)}) copy-start(bf16[4096,384]{1,0:T(8,128)(2,1)} %param.9) | copy-start | bytes 9437188
  6.5 159.6 %copy-start.4 = (f32[384]{0:T(512)S(1)}, f32[384]{0:T(512)}, u32[]{:S(2)}) copy-start(f32[384]{0:T(512)} %param.11) | copy-start | bytes 4612
  28.2 13.5 %all-to-all-start = ((s32[16,1,12]{2,1,0:T(1,128)}), s32[16,1,12]{2,1,0:T(1,128)S(1)}, u32[]{:S(2)}, u32[]{:S(2)}) async-start(s32[16,1,12]{2,1,0:T(1,128)} %bitcast.10), calls=%async_computation | async-start | bytes 16384 | tf_op jit(solution)/shard_map/all_to_all | solution.py:63
  35.3 130.8 %all-reduce.2.cloned.1.call-start = ((), (), s32[]{:S(2)}) async-start(), calls=%async_computation.3 | async-start | bytes 196608 | tf_op jit(solution)/shard_map/psum | solution.py:37
  37.8 0.8 copy-start.1
  39.8 128.4 %copy-start.3 = (f32[4096]{0:T(1024)S(1)}, f32[4096]{0:T(1024)}, u32[]{:S(2)}) copy-start(f32[4096]{0:T(1024)} %param.10) | copy-start | bytes 49156
  39.9 257.7 %reduce-scatter.2.cloned.1.call-start = ((), (), s32[]{:S(2)}) async-start(), calls=%async_computation.4 | async-start | bytes 98304 | tf_op jit(solution)/shard_map/reduce_scatter | solution.py:74
  166.1 2.1 copy-start.2
  254.2 3.1 %copy-start.5 = (f32[256]{0:T(256)S(1)}, f32[256]{0:T(256)}, u32[]{:S(2)}) copy-start(f32[256]{0:T(256)} %param.17) | copy-start | bytes 3076
Sparse Core Ops, SparseCore 0:
  41.7 124.3 all-reduce.1
  257.5 9.7 reduce-scatter.1
where the time goes:
time: 307 us; the launch traced here: 306 us
  waiting for transfers between devices  126 us (41%)
  blocking collectives  116 us (38%)
  local copies, waits for them, and re-layouts  31.1 us (10%)
  between operations  13.5 us (4%)
  matrix products  7.3 us (2%)
  starting transfers between devices  7.19 us (2%)
  other arithmetic  4.24 us (1%)
    psum x1, waiting for transfers between devices, body(): projection = lax.psum(partial_proj, ('ex', 'feat'))  124 us
    all_to_all x1, blocking collectives, body(): lax.all_to_all(fetched, 'ex', split_axis=0, concat_axis=0, tiled=True)  76.2 us
    psum x1, blocking collectives, body(): lax.psum(jnp.sum(test_wide * exact_dir, axis=(0, 2)), ('ex', 'feat'))  40.1 us
    scatter x1, local copies, waits for them, and re-layouts, body(): requests = jnp.full((ex_devices, capacity), -1, jnp.int32).at[targets, sl...  18.5 us
    all_to_all x1, starting transfers between devices, body(): lax.all_to_all(requests, 'ex', split_axis=0, concat_axis=0, tiled=True)  7.11 us
  transfers between devices with their start and end apart: 3, of which 2 were waited for; matrix products, arithmetic and copies ran while one was open for 1% of the time, Pallas kernels for 0%

commit v1 on v0

--- a/solution.py
+++ b/solution.py
@@ -39,7 +39,8 @@
     exact_dir = diag_tiles[:, None, :] * test_wide + jnp.einsum(
         "afr,tr->atf", basis_tiles, scaled_proj, preferred_element_type=jnp.float32
     )
-    self_inf = lax.psum(jnp.sum(test_wide * exact_dir, axis=(0, 2)), ("ex", "feat"))
+    vec = jnp.sum(test_wide * exact_dir, axis=(0, 2))
+    self_inf = lax.psum(lax.psum(vec, "feat"), "ex")
     direction = exact_dir.astype(jnp.bfloat16)
     blocks_here = train_tiles.shape[0]
     slots_here = train_tiles.shape[1]

time: 307 us -> 304 us (level)
    psum x1 -> x2, blocking collectives: 40.1 us -> 37.1 us  [body(): self_inf = lax.psum(lax.psum(vec, 'feat'), 'ex')]
where the time goes in v1:
time: 304 us; the launch traced here: 303 us
  waiting for transfers between devices  126 us (41%)
  blocking collectives  113 us (37%)
  local copies, waits for them, and re-layouts  31.1 us (10%)
  between operations  13.5 us (4%)
  matrix products  7.3 us (2%)
  starting transfers between devices  7.19 us (2%)
  other arithmetic  4.24 us (1%)
    psum x1, waiting for transfers between devices, body(): projection = lax.psum(partial_proj, ('ex', 'feat'))  124 us
    all_to_all x1, blocking collectives, body(): lax.all_to_all(fetched, 'ex', split_axis=0, concat_axis=0, tiled=True)  76.2 us
    psum x2, blocking collectives, body(): self_inf = lax.psum(lax.psum(vec, 'feat'), 'ex')  37.1 us
    scatter x1, local copies, waits for them, and re-layouts, body(): requests = jnp.full((ex_devices, capacity), -1, jnp.int32).at[targets, sl...  18.5 us
    all_to_all x1, starting transfers between devices, body(): lax.all_to_all(requests, 'ex', split_axis=0, concat_axis=0, tiled=True)  7.11 us
  transfers between devices with their start and end apart: 3, of which 2 were waited for; matrix products, arithmetic and copies ran while one was open for 1% of the time, Pallas kernels for 0%

profile of v1, /device:TPU:0, one launch (start us, length us, event | category | flops | bytes accessed | tf_op | source)
XLA Modules:
  0.0 302.8 jit_solution(14479934108966226162)
XLA Ops:
  6.5 0.9 copy.25
  7.4 0.1 reshape.251
  7.5 0.1 reshape.250
  7.6 0.7 iota_compare_fusion.3
  8.4 0.1 lt.83
  8.5 0.1 lt.81
  8.6 0.1 fusion.11
  8.7 0.2 reduce_window_sum.11
  8.9 0.2 select_reduce_fusion
  9.1 0.6 broadcast_in_dim.15
  9.7 18.5 %scatter_fusion = s32[16,12]{1,0:T(8,128)} fusion(s32[16,12]{1,0:T(8,128)} %broadcast_in_dim.15, s32[128]{0:T(128)S(1)} %fusion.21, s32[128]{0:T(128)S(1)} %get-tuple-element.9), kind=kCustom, calls=%fused_computation.2 | custom fusion | bytes 2560 | tf_op jit(solution)/shard_map/scatter | solution.py:61
  28.2 7.1 %all-to-all-start = ((s32[16,1,12]{2,1,0:T(1,128)}), s32[16,1,12]{2,1,0:T(1,128)S(1)}, u32[]{:S(2)}, u32[]{:S(2)}) async-start(s32[16,1,12]{2,1,0:T(1,128)} %bitcast.10), calls=%async_computation | async-start | bytes 16384 | tf_op jit(solution)/shard_map/all_to_all | solution.py:64
  35.4 0.7 broadcast_subtract_fusion
  36.1 0.1 copy.22
  36.2 1.6 fusion.3
  37.8 0.8 copy-done.1
  38.6 1.3 convolution_bitcast_fusion
  39.9 1.8 all-to-all-done
  41.7 0.1 reshape.255
  41.8 124.3 %all-reduce.2.cloned.1.call-done = f32[64,384]{1,0:T(8,128)} async-done(((f32[64,384]{1,0:T(8,128)}), f32[64,384]{1,0:T(8,128)}) %all-reduce.2.cloned.1.call-update) | async-done | bytes 98320 | tf_op jit(solution)/shard_map/psum | solution.py:37
  166.1 2.0 fusion.13
  168.2 0.8 fusion.5
  169.0 1.0 copy.28
  170.0 3.8 %gather_fusion = bf16[192,64,128]{2,1,0:T(8,128)(2,1)} fusion(bf16[32,64,128]{2,1,0:T(8,128)(2,1)} %copy.28, s32[1024]{0:T(1024)S(1)} %pad_clamp_fusion), kind=kCustom, calls=%fused_computation | custom fusion | bytes 6292224 | tf_op jit(solution)/shard_map/gather | solution.py:63
  173.8 76.2 %all_to_all.14 = bf16[16,12,64,128]{3,2,1,0:T(8,128)(2,1)} all-to-all(bf16[16,12,64,128]{3,2,1,0:T(8,128)(2,1)} %bitcast.43), channel_id=1, replica_groups=mesh['ex'=16,'feat'=2] {'ex'}, dimensions={0} | all-to-all | bytes 6291456 | tf_op jit(solution)/shard_map/all_to_all | solution.py:66
  250.0 4.2 %gather_fusion.1 = bf16[128,64,128]{2,1,0:T(8,128)(2,1)} fusion(bf16[16,12,64,128]{3,2,1,0:T(8,128)(2,1)} %all_to_all.14, s32[128]{0:T(128)S(1)} %get-tuple-element.5), kind=kCustom, calls=%fused_computation.1 | custom fusion | bytes 4195328 | tf_op jit(solution)/shard_map/gather | solution.py:68
  254.2 2.4 fusion
  256.6 0.7 copy.29
  257.4 5.0 %psum.22 = f32[64]{0:T(128)S(1)} all-reduce(f32[64]{0:T(128)S(1)} %get-tuple-element.7), channel_id=1, replica_groups=mesh['ex'=16,'feat'=2] {'feat'}, use_global_device_ids=true, to_apply=%region_6.7 | all-reduce | flops 64 | bytes 512 | tf_op jit(solution)/shard_map/psum | solution.py:43
  262.4 32.1 %psum.23 = f32[64]{0:T(128)S(1)} all-reduce(f32[64]{0:T(128)S(1)} %psum.22), channel_id=1, replica_groups=mesh['ex'=16,'feat'=2] {'ex'}, use_global_device_ids=true, to_apply=%region_7.8 | all-reduce | flops 64 | bytes 512 | tf_op jit(solution)/shard_map/psum | solution.py:43
  294.5 0.1 dynamic-slice_sqrt_fusion
  294.6 1.5 multiply_divide_fusion
  (22 shorter events, 0.2 us)
Async XLA Ops:
  6.5 31.2 %copy-start = (bf16[4096,384]{1,0:T(8,128)(2,1)S(1)}, bf16[4096,384]{1,0:T(8,128)(2,1)}, u32[]{:S(2)}) copy-start(bf16[4096,384]{1,0:T(8,128)(2,1)} %param.9) | copy-start | bytes 9437188
  6.5 159.6 %copy-start.4 = (f32[384]{0:T(512)S(1)}, f32[384]{0:T(512)}, u32[]{:S(2)}) copy-start(f32[384]{0:T(512)} %param.11) | copy-start | bytes 4612
  28.2 13.5 %all-to-all-start = ((s32[16,1,12]{2,1,0:T(1,128)}), s32[16,1,12]{2,1,0:T(1,128)S(1)}, u32[]{:S(2)}, u32[]{:S(2)}) async-start(s32[16,1,12]{2,1,0:T(1,128)} %bitcast.10), calls=%async_computation | async-start | bytes 16384 | tf_op jit(solution)/shard_map/all_to_all | solution.py:64
  35.3 130.8 %all-reduce.2.cloned.1.call-start = ((), (), s32[]{:S(2)}) async-start(), calls=%async_computation.3 | async-start | bytes 196608 | tf_op jit(solution)/shard_map/psum | solution.py:37
  37.8 0.8 copy-start.1
  39.8 128.4 %copy-start.3 = (f32[4096]{0:T(1024)S(1)}, f32[4096]{0:T(1024)}, u32[]{:S(2)}) copy-start(f32[4096]{0:T(1024)} %param.10) | copy-start | bytes 49156
  39.9 254.7 %reduce-scatter.2.cloned.1.call-start = ((), (), s32[]{:S(2)}) async-start(), calls=%async_computation.4 | async-start | bytes 98304 | tf_op jit(solution)/shard_map/reduce_scatter | solution.py:75
  166.1 2.1 copy-start.2
  254.2 3.1 %copy-start.5 = (f32[256]{0:T(256)S(1)}, f32[256]{0:T(256)}, u32[]{:S(2)}) copy-start(f32[256]{0:T(256)} %param.17) | copy-start | bytes 3076
Sparse Core Ops, SparseCore 0:
  41.7 124.3 all-reduce.1
  257.5 9.6 reduce-scatter.1
